TPU v7x, 32 devices: a whole 2x2x4 slice. The times are simulated.
32 devices in a mesh: pb: 8 (over y, x, core), row: 4 (over z).
Axes of the slice: x: 2, y: 2, z: 4, core: 2. Of those that a mesh axis runs over, the one named last changes fastest.
Arguments:
- screened: bfloat16 [16, 2, 1024, 1024], P('pb', None, 'row'), may hold values from -1.0546875 to 1.0546875
- response: bfloat16 [16, 2, 1024, 1024], P(None, None, 'pb', 'row'), may hold values from -0.1875 to 0.1875
- q_owner: int32 [16], replicated, may hold values from 0 to 15, each once
- g_index: int32 [16, 1024], P('pb'), may hold values from 0 to 1023, each once within a row
Outputs:
- tangent: float32 [16, 2, 1024, 1024], P(None, None, ('row', 'pb'))
Inputs may be any that keep to these rules, and one draw needn't show every extreme that they name: `q_owner`: each owner slot appears once. `g_index`: each row is a permutation of the 1024 plane waves.
All inputs are finite; a program needn't handle non-finite values.
Results may differ from a plain program's by a relative error of at most 0.0029.
Values may be sent and summed in bfloat16 or wider, within the bound.
A program may use at most 64 MiB of HBM per device.

v0:
```python
import jax
import jax.numpy as jnp
from jax import lax
from jax.sharding import PartitionSpec as P


def complex_product(left, right):

    def product(first, second):
        return jnp.einsum("qik,qkj->qij", first, second, preferred_element_type=jnp.float32)

    real_part = product(left[:, 0], right[:, 0]) - product(left[:, 1], right[:, 1])
    imag_part = product(left[:, 0], right[:, 1]) + product(left[:, 1], right[:, 0])
    return jnp.stack((real_part, imag_part), axis=1)


def body(screened, response, q_owner, g_index):
    slot_count = q_owner.shape[0]
    inverse = (
        jnp.zeros((slot_count,), jnp.int32).at[q_owner].set(jnp.arange(slot_count, dtype=jnp.int32))
    )
    ordered = jnp.take(response, inverse, axis=0)
    at_owner = lax.all_to_all(ordered, "pb", split_axis=0, concat_axis=2, tiled=True)
    permuted = jax.vmap(lambda block, table: block[:, table, :])(at_owner, g_index)
    whole = lax.all_gather(screened, "row", axis=2, tiled=True)
    column_half = complex_product(whole, permuted).astype(jnp.bfloat16)
    halfway = lax.all_to_all(column_half, "row", split_axis=2, concat_axis=3, tiled=True)
    result = complex_product(halfway, whole)
    returned = lax.all_to_all(result, "pb", split_axis=2, concat_axis=0, tiled=True)
    return jnp.take(returned, q_owner, axis=0)


def solution(mesh):
    return jax.shard_map(
        body,
        mesh=mesh,
        in_specs=(P("pb", None, "row", None), P(None, None, "pb", "row"), P(), P("pb", None)),
        out_specs=P(None, None, ("row", "pb"), None),
        check_vma=False,
    )
```

profile of v0, /device:TPU:11, one launch (start us, length us, event | category | flops | bytes accessed | tf_op | source)
XLA Modules:
  0.0 323.3 jit_solution(15050981554449693041)
XLA Ops:
  6.5 3.2 copy.32
  9.8 0.6 copy-done.4
  10.4 0.6 scatter_custom_fusion
  11.1 2.0 gather_fusion
  13.1 3.2 broadcast_select_fusion.1
  16.3 5.2 %all-to-all-start = ((bf16[16,2,128,256]{3,2,1,0:T(8,128)(2,1)}), bf16[16,2,128,256]{3,2,1,0:T(8,128)(2,1)}, u32[]{:S(2)}, u32[]{:S(2)}) async-start(bf16[16,2,128,256]{3,2,1,0:T(8,128)(2,1)} %broadcast_select_fusion.1), calls=%async_computation | async-start | bytes 4194304 | tf_op jit(solution)/shard_map/all_to_all | solution.py:23
  21.6 25.1 %all-to-all-done = bf16[16,2,128,256]{3,2,1,0:T(8,128)(2,1)} async-done(((bf16[16,2,128,256]{3,2,1,0:T(8,128)(2,1)}), bf16[16,2,128,256]{3,2,1,0:T(8,128)(2,1)}, u32[]{:S(2)}, u32[]{:S(2)}) %all-to-all-start) | async-done | bytes 2097184 | tf_op jit(solution)/shard_map/all_to_all | solution.py:23
  46.7 1.7 copy.28
  48.4 3.5 %copy.29 = bf16[2,2,1024,256]{3,1,2,0:T(2,128)(2,1)} copy(bf16[2,2,1024,256]{3,2,1,0:T(8,128)(2,1)S(1)} %bitcast.86) | data formatting | bytes 4194304 | tf_op jit(solution)/shard_map/all_to_all | solution.py:23
  52.0 20.5 %gather_fusion.2 = bf16[2048,2,256]{2,1,0:T(2,128)(2,1)} fusion(bf16[2,2,1024,256]{3,1,2,0:T(2,128)(2,1)} %copy.29, s32[2048]{0:T(1024)S(1)} %bitcast.80), kind=kCustom, calls=%fused_computation.2 | custom fusion | bytes 4210688 | tf_op jit(solution)/shard_map/vmap()/gather | solution.py:24
  72.4 4.7 %copy.31 = bf16[2,1024,2,256]{1,3,0,2:T(8,128)(2,1)S(1)} copy(bf16[2,1024,2,256]{3,2,1,0:T(2,128)(2,1)} %bitcast.85) | data formatting | bytes 4194304 | tf_op jit(solution)/shard_map/vmap()/gather | solution.py:24
  77.2 80.6 %all-gather.2.cloned.1.call-done = bf16[2,2,1024,1024]{3,2,0,1:T(8,128)(2,1)} async-done(((bf16[2,2,256,1024]{3,2,0,1:T(8,128)(2,1)}), bf16[2,2,1024,1024]{3,2,0,1:T(8,128)(2,1)}) %all-gather.2.cloned.1.call-update) | async-done | bytes 8388624 | tf_op jit(solution)/shard_map/all_gather | solution.py:25
  157.8 3.6 %fusion.3 = f32[2,256,1024]{2,1,0:T(8,128)S(1)} fusion(bf16[2,2,1024,1024]{3,2,0,1:T(8,128)(2,1)} %all-gather.2.cloned.1.call-done, bf16[2,2,1024,256]{2,3,0,1:T(8,128)(2,1)S(1)} %bitcast.89), kind=kOutput, calls=%fused_computation.10 | convolution fusion | flops 1073741824 | bytes 7340032 | tf_op jit(solution)/shard_map/qik,qkj->qij/dot_general | solution.py:10
  161.4 1.0 copy-done.2
  162.4 1.4 fusion.2
  163.8 1.4 fusion.8
  165.2 1.4 fusion.9
  166.9 4.0 %copy.33 = bf16[2,2,1024,256]{3,0,1,2:T(2,128)(2,1)} copy(bf16[2,2,1024,256]{2,3,0,1:T(8,128)(2,1)S(1)} %pad_maximum_fusion.1) | data formatting | bytes 4194304 | tf_op jit(solution)/shard_map/stack | solution.py:14
  170.9 52.8 %all_to_all.54 = bf16[2,2,1024,256]{3,0,1,2:T(2,128)(2,1)S(1)} all-to-all(bf16[2,2,1024,256]{3,0,1,2:T(2,128)(2,1)} %copy.33), channel_id=1, replica_groups=mesh['pb'=8,'row'=4] {'row'}, dimensions={2} | all-to-all | bytes 4194304 | tf_op jit(solution)/shard_map/all_to_all | solution.py:27
  223.7 2.9 copy.43
  226.7 3.2 all_to_all.46
  229.9 3.6 %fusion.1 = f32[2,256,1024]{2,1,0:T(8,128)S(1)} fusion(bf16[2,2,1024,1024]{3,2,0,1:T(8,128)(2,1)} %all-gather.2.cloned.1.call-done, bf16[2,2,256,1024]{3,2,0,1:T(8,128)(2,1)S(1)} %all_to_all.46), kind=kOutput, calls=%fused_computation.8 | convolution fusion | flops 1073741824 | bytes 7340032 | tf_op jit(solution)/shard_map/qik,qkj->qij/dot_general | solution.py:10
  233.5 3.6 %fusion = f32[2,256,1024]{2,1,0:T(8,128)S(1)} fusion(bf16[2,2,1024,1024]{3,2,0,1:T(8,128)(2,1)} %all-gather.2.cloned.1.call-done, bf16[2,2,256,1024]{3,2,0,1:T(8,128)(2,1)S(1)} %all_to_all.46), kind=kOutput, calls=%fused_computation.7 | convolution fusion | flops 1073741824 | bytes 7340032 | tf_op jit(solution)/shard_map/qik,qkj->qij/dot_general | solution.py:10
  237.2 1.3 subtract_bitcast_fusion
  238.5 1.3 add_bitcast_fusion
  240.1 5.2 %copy.35 = f32[2,2,256,1024]{3,0,1,2:T(2,128)} copy(f32[2,2,256,1024]{3,2,0,1:T(8,128)S(1)} %pad_maximum_fusion) | data formatting | bytes 8388608 | tf_op jit(solution)/shard_map/stack | solution.py:14
  245.4 6.3 %all-to-all-start.2 = ((f32[2,2,256,1024]{3,0,1,2:T(2,128)}), f32[2,2,256,1024]{3,0,1,2:T(2,128)}, u32[]{:S(2)}, u32[]{:S(2)}) async-start(f32[2,2,256,1024]{3,0,1,2:T(2,128)} %copy.35), calls=%async_computation.2 | async-start | bytes 8388608 | tf_op jit(solution)/shard_map/all_to_all | solution.py:29
  251.7 47.6 %all-to-all-done.2 = f32[2,2,256,1024]{3,0,1,2:T(2,128)} async-done(((f32[2,2,256,1024]{3,0,1,2:T(2,128)}), f32[2,2,256,1024]{3,0,1,2:T(2,128)}, u32[]{:S(2)}, u32[]{:S(2)}) %all-to-all-start.2) | async-done | bytes 4194336 | tf_op jit(solution)/shard_map/all_to_all | solution.py:29
  299.3 4.6 %copy.36 = f32[2,2,256,1024]{3,2,1,0:T(8,128)S(1)} copy(f32[2,2,256,1024]{3,0,1,2:T(2,128)} %all-to-all-done.2) | data formatting | bytes 8388608 | tf_op jit(solution)/shard_map/all_to_all | solution.py:29
  303.9 2.3 copy.37
  306.3 4.9 %gather_fusion.1 = f32[16,2,32,1024]{3,2,1,0:T(8,128)} fusion(f32[16,2,32,1024]{3,2,1,0:T(8,128)} %bitcast.81, s32[1024]{0:T(1024)S(1)} %pad_clamp_fusion), kind=kCustom, calls=%fused_computation.1 | custom fusion | bytes 8388672 | tf_op jit(solution)/shard_map/jit(_take)/gather | solution.py:30
  311.2 5.3 %broadcast_select_fusion = f32[16,2,32,1024]{3,2,1,0:T(8,128)} fusion(f32[16,2,32,1024]{3,2,1,0:T(8,128)} %gather_fusion.1, pred[16]{0:T(512)(128)(4,1)S(1)} %compare_and_fusion.1), kind=kLoop, calls=%fused_computation.17 | loop fusion | flops 1048576 | bytes 8388624 | tf_op jit(solution)/shard_map/jit(_take)/select_n | solution.py:30
  (26 shorter events, 0.6 us)
Async XLA Ops:
  6.5 4.6 %copy-start = (bf16[16,2,128,256]{3,2,1,0:T(8,128)(2,1)S(1)}, bf16[16,2,128,256]{3,2,1,0:T(8,128)(2,1)}, u32[]{:S(2)}) copy-start(bf16[16,2,128,256]{3,2,1,0:T(8,128)(2,1)} %param.5) | copy-start | bytes 6291460
  6.5 151.2 %all-gather.2.cloned.1.call-start = ((), (), s32[]{:S(2)}) async-start(), calls=%async_computation.3 | async-start | bytes 10485760 | tf_op jit(solution)/shard_map/all_gather | solution.py:25
  9.8 0.7 copy-start.4
  16.3 5.2 %copy-start.3 = (s32[2,1024]{1,0:T(2,128)S(1)}, s32[2,1024]{1,0:T(2,128)}, u32[]{:S(2)}) copy-start(s32[2,1024]{1,0:T(2,128)} %param.7) | copy-start | bytes 24580
  16.3 30.4 %all-to-all-start = ((bf16[16,2,128,256]{3,2,1,0:T(8,128)(2,1)}), bf16[16,2,128,256]{3,2,1,0:T(8,128)(2,1)}, u32[]{:S(2)}, u32[]{:S(2)}) async-start(bf16[16,2,128,256]{3,2,1,0:T(8,128)(2,1)} %broadcast_select_fusion.1), calls=%async_computation | async-start | bytes 4194304 | tf_op jit(solution)/shard_map/all_to_all | solution.py:23
  157.8 4.6 %copy-start.2 = (bf16[2,2,1024,1024]{3,2,0,1:T(8,128)(2,1)S(1)}, bf16[2,2,1024,1024]{3,2,0,1:T(8,128)(2,1)}, u32[]{:S(2)}) copy-start(bf16[2,2,1024,1024]{3,2,0,1:T(8,128)(2,1)} %all-gather.2.cloned.1.call-done) | copy-start | bytes 25165828
  229.9 7.2 %slice-start = ((s8[8388608]{0:T(1024)(128)(4,1)}), s8[4194304]{0:T(1024)(128)(4,1)S(1)}, s32[]{:S(2)}) async-start(s8[8388608]{0:T(1024)(128)(4,1)} %bitcast.83), calls=%async_computation.4 | async-start | bytes 8388608
  233.5 3.6 %slice-start.1 = ((s8[8388608]{0:T(1024)(128)(4,1)}), s8[4194304]{0:T(1024)(128)(4,1)S(1)}, s32[]{:S(2)}) async-start(s8[8388608]{0:T(1024)(128)(4,1)} %bitcast.83), calls=%async_computation.5 | async-start | bytes 8388608
  245.4 54.0 %all-to-all-start.2 = ((f32[2,2,256,1024]{3,0,1,2:T(2,128)}), f32[2,2,256,1024]{3,0,1,2:T(2,128)}, u32[]{:S(2)}, u32[]{:S(2)}) async-start(f32[2,2,256,1024]{3,0,1,2:T(2,128)} %copy.35), calls=%async_computation.2 | async-start | bytes 8388608 | tf_op jit(solution)/shard_map/all_to_all | solution.py:29
  311.2 5.3 %copy-start.1 = (bf16[16,2,128,256]{3,2,1,0:T(8,128)(2,1)S(1)}, bf16[16,2,128,256]{3,2,1,0:T(8,128)(2,1)}, u32[]{:S(2)}) copy-start(bf16[16,2,128,256]{3,2,1,0:T(8,128)(2,1)} %param.5) | copy-start | bytes 6291460
Sparse Core Ops, SparseCore 0:
  9.9 147.8 all-gather.1
where the time goes:
time: 328 us; the launch traced here: 323 us
  waiting for transfers between devices  153 us (47%)
  local copies, waits for them, and re-layouts  65.4 us (20%)
  blocking collectives  52.8 us (16%)
  matrix products  17.6 us (5%)
  between operations  13.6 us (4%)
  starting transfers between devices  11.5 us (4%)
  other arithmetic  9.02 us (3%)
    all_gather x1, waiting for transfers between devices, body(): whole = lax.all_gather(screened, 'row', axis=2, tiled=True)  80.6 us
    all_to_all x1, blocking collectives, body(): lax.all_to_all(column_half, 'row', split_axis=2, concat_axis=3, tiled=True)  52.8 us
    all_to_all x1, waiting for transfers between devices, body(): lax.all_to_all(result, 'pb', split_axis=2, concat_axis=0, tiled=True)  47.6 us
    gather x2, local copies, waits for them, and re-layouts, body(): block[:, table, :]  25.2 us
    all_to_all x1, waiting for transfers between devices, body(): lax.all_to_all(ordered, 'pb', split_axis=0, concat_axis=2, tiled=True)  25.1 us
    dot_general x8, matrix products, product(): jnp.einsum('qik,qkj->qij', first, second, preferred_element_type=jnp.floa...  17.6 us
    another operation x2, local copies, waits for them, and re-layouts, complex_product(): return jnp.stack((real_part, imag_part), axis=1)  9.3 us
    all_to_all x2, local copies, waits for them, and re-layouts, body(): lax.all_to_all(result, 'pb', split_axis=2, concat_axis=0, tiled=True)  6.94 us
  transfers between devices with their start and end apart: 3, of which 3 were waited for; matrix products, arithmetic and copies ran while one was open for 11% of the time, Pallas kernels for 0%

commit v1 on v0

v1 whole, which is shorter than its diff:
```python
import functools

import jax
import jax.numpy as jnp
from jax import lax
from jax.experimental import pallas as pl
from jax.experimental.pallas import tpu as pltpu
from jax.sharding import PartitionSpec as P

F32 = jnp.float32
BF16 = jnp.bfloat16


def to_slots(order, source, target):
    target[...] = source[...]


def from_slots(order, source, target):
    target[...] = source[...].astype(target.dtype)


def team_kernel(
    pb, rows, team, tile,
    response, screened, table, out,
    raw, weight, chi, owner_table, half, half_out, stage,
    chi_sent, chi_got, w_sent, w_got, f_sent, f_got, g_sent, g_got, h_sent, h_got, o_sent, o_got,
):
    slots = response.shape[0]
    per_pb = screened.shape[0]
    size = screened.shape[3]
    groups = pb // team
    block_rows, block_cols = response.shape[2], response.shape[3]
    own_cols = size // team
    w_rows = size // rows
    w_part = w_rows // team
    spread = rows // team
    dests = pb // team
    out_rows = out.shape[2]
    near = rows // 2

    p, r = lax.axis_index("pb"), lax.axis_index("row")
    t, group = p % team, p // team
    slot = group * rows + r

    def same(a, b):
        return jnp.logical_and(a == p, b == r)

    barrier = pltpu.get_barrier_semaphore()

    def greet(k, carry):
        @pl.when(k != p * rows + r)
        def _():
            pl.semaphore_signal(barrier, inc=1, device_id=(k // rows, k % rows), device_id_type=pl.DeviceIdType.MESH)
        return carry

    lax.fori_loop(0, pb * rows, greet, 0)
    pl.semaphore_wait(barrier, pb * rows - 1)

    def send(src, dst, sent, got, at_p, at_r):
        @pl.when(same(at_p, at_r))
        def _():
            pltpu.make_async_copy(src, dst, got).start()

        @pl.when(jnp.logical_not(same(at_p, at_r)))
        def _():
            remote(src, dst, sent, got, at_p, at_r).start()

    def remote(src, dst, sent, got, at_p, at_r):
        return pltpu.make_async_remote_copy(
            src_ref=src, dst_ref=dst, send_sem=sent, recv_sem=got,
            device_id=(at_p, at_r), device_id_type=pl.DeviceIdType.MESH,
        )

    def arrived(ref, sem):
        pltpu.make_async_copy(ref, ref, sem).wait()

    def left(ref, sem, at_p, at_r):
        @pl.when(jnp.logical_not(same(at_p, at_r)))
        def _():
            pltpu.make_async_copy(ref, ref, sem).wait()

    def far_first(k):
        side = r // near
        across = (1 - side) * near + (r + k) % near
        beside = side * near + (r + 1 + k) % near
        return jnp.where(k < near, across, beside)

    holder = r // per_pb
    mine = table.at[r % per_pb]

    @pl.when(t == holder)
    def _():
        pltpu.make_async_copy(mine, owner_table, g_got).start()
        for step in range(1, team):
            remote(mine, owner_table, g_sent.at[step - 1], g_got, group * team + (t + step) % team, r).start()

    member = r // spread

    def chi_place(k):
        at_r = far_first(k // groups)
        at_group = (group + k) % groups
        return at_group * rows + at_r, at_group * team + member, at_r

    def chi_target(from_p, from_r):
        return raw.at[
            :,
            pl.ds(pl.multiple_of(from_p * block_rows, block_rows), block_rows),
            pl.ds(pl.multiple_of((from_r % spread) * block_cols, block_cols), block_cols),
        ]

    def chi_send(k, carry):
        number, at_p, at_r = chi_place(k)
        send(response.at[number], chi_target(p, r), chi_sent.at[k], chi_got.at[p * spread + r % spread], at_p, at_r)
        return carry

    lax.fori_loop(0, slots, chi_send, 0)

    def w_target(block, part):
        start = pl.multiple_of(block * w_rows + part * w_part, w_part)
        return weight.at[:, pl.ds(start, w_part), :]

    def w_place(k):
        i, part = k // team, k % team
        return i, part, group * team + part, t * per_pb + i

    def w_send(k, carry):
        i, part, at_p, at_r = w_place(k)
        src = screened.at[i, :, pl.ds(pl.multiple_of(part * w_part, w_part), w_part), :]
        send(src, w_target(r, part), w_sent.at[k], w_got.at[r], at_p, at_r)
        return carry

    lax.fori_loop(0, per_pb * team, w_send, 0)

    arrived(owner_table, g_got)

    def chi_wait(k, carry):
        arrived(chi_target(k // spread, k % spread), chi_got.at[k])
        return carry

    lax.fori_loop(0, pb * spread, chi_wait, 0)

    def reorder(k, carry):
        start = pl.multiple_of(k * tile, tile)
        wanted = owner_table[:, pl.ds(start, tile)]
        chosen = (lax.broadcasted_iota(jnp.int32, (size, tile), 0) == wanted).astype(F32).astype(BF16)
        for part in range(2):
            chi[part, pl.ds(start, tile), :] = lax.dot_general(
                chosen, raw[part], (((0,), (0,)), ((), ())), preferred_element_type=F32
            ).astype(BF16)
        return carry

    lax.fori_loop(0, size // tile, reorder, 0)

    def forward(block, step):
        at_p = group * team + (t + step) % team
        ref = w_target(block, t)
        return remote(ref, ref, f_sent.at[block * team + step], f_got.at[block * team + step], at_p, r)

    def pass_on(k, carry):
        block = (r + k) % rows
        arrived(w_target(block, t), w_got.at[block])
        for step in range(1, team):
            forward(block, step).start()
        return carry

    def hand(block, step):
        at_p = group * team + (t + step) % team
        return remote(
            half_out.at[step - 1, block], half.at[t, block],
            h_sent.at[block * team + step], h_got.at[block * team + step], at_p, r,
        )

    width = min(tile, own_cols)

    def first(k, carry):
        block = (r + k) % rows
        pass_on(k, carry)
        for step in range(1, team):
            arrived(w_target(block, (t + team - step) % team), f_got.at[block * team + step])
        for step in range(team):
            part = (t + step) % team
            start = pl.multiple_of(block * w_rows + part * w_part, w_part)
            both = jnp.concatenate(
                (weight[0, pl.ds(start, w_part), :], weight[1, pl.ds(start, w_part), :]), axis=0
            )
            for c in range(own_cols // width):
                cols = slice(c * width, (c + 1) * width)
                by_real = jnp.dot(both, chi[0, :, cols], preferred_element_type=F32)
                by_imag = jnp.dot(both, chi[1, :, cols], preferred_element_type=F32)
                real = (by_real[:w_part] - by_imag[w_part:]).astype(BF16)
                imag = (by_imag[:w_part] + by_real[w_part:]).astype(BF16)
                value = jnp.concatenate((real, imag), axis=0)
                if step == 0:
                    half[t, block, :, cols] = value
                else:
                    half_out[step - 1, block, :, cols] = value
        for step in range(1, team):
            hand(block, step).start()
        return carry

    lax.fori_loop(0, rows, first, 0)

    def out_send(k, m):
        at_r = far_first(k)
        send(stage.at[at_r, m], out.at[slot], o_sent.at[at_r * dests + m], o_got.at[slot], t * dests + m, at_r)

    def second(k, carry):
        block = far_first(k)
        for step in range(1, team):
            arrived(half.at[(t + team - step) % team, block], h_got.at[block * team + step])

        def columns(c, inner):
            start = pl.multiple_of(c * tile, tile)
            by_real = jnp.zeros((2 * w_part, tile), F32)
            by_imag = jnp.zeros((2 * w_part, tile), F32)
            for source in range(team):
                left_side = half[source, block]
                deep = slice(source * own_cols, (source + 1) * own_cols)
                by_real += jnp.dot(left_side, weight[0, deep, pl.ds(start, tile)], preferred_element_type=F32)
                by_imag += jnp.dot(left_side, weight[1, deep, pl.ds(start, tile)], preferred_element_type=F32)
            real = (by_real[:w_part] - by_imag[w_part:]).astype(BF16)
            imag = (by_imag[:w_part] + by_real[w_part:]).astype(BF16)
            for m in range(dests):
                lines = slice(m * out_rows, (m + 1) * out_rows)
                stage[block, m, 0, :, pl.ds(start, tile)] = real[lines]
                stage[block, m, 1, :, pl.ds(start, tile)] = imag[lines]
            return inner

        lax.fori_loop(0, size // tile, columns, 0)

        @pl.when(k > 0)
        def _():
            for m in range(dests):
                out_send(k - 1, m)
        return carry

    lax.fori_loop(0, rows, second, 0)
    for m in range(dests):
        out_send(rows - 1, m)

    def out_wait(k, carry):
        arrived(out.at[k], o_got.at[k])
        return carry

    lax.fori_loop(0, slots, out_wait, 0)

    @pl.when(t == holder)
    def _():
        for step in range(1, team):
            pltpu.make_async_copy(mine, mine, g_sent.at[step - 1]).wait()

    def chi_left(k, carry):
        number, at_p, at_r = chi_place(k)
        left(response.at[number], chi_sent.at[k], at_p, at_r)
        return carry

    lax.fori_loop(0, slots, chi_left, 0)

    def w_left(k, carry):
        i, part, at_p, at_r = w_place(k)
        left(w_target(r, part), w_sent.at[k], at_p, at_r)
        return carry

    lax.fori_loop(0, per_pb * team, w_left, 0)

    def blocks_left(block, carry):
        for step in range(1, team):
            forward(block, step).wait_send()
            hand(block, step).wait_send()
        for m in range(dests):
            left(stage.at[block, m], o_sent.at[block * dests + m], t * dests + m, block)
        return carry

    lax.fori_loop(0, rows, blocks_left, 0)


def body(pb, rows, screened, response, q_owner, g_index):
    slots, _, block_rows, block_cols = response.shape
    per_pb, size = screened.shape[0], screened.shape[3]
    team = pb * rows // slots
    own_cols = size // team
    w_part = size // rows // team
    out_rows = size // (pb * rows)
    dests = pb // team
    spread = rows // team
    tile = min(256, size)

    def reordered(kernel, array, dtype, back):
        shape = (1,) + array.shape[1:]
        here = lambda q, order: (q, 0, 0, 0)
        there = lambda q, order: (order[q], 0, 0, 0)
        return pl.pallas_call(
            kernel,
            out_shape=jax.ShapeDtypeStruct(array.shape, dtype),
            grid_spec=pltpu.PrefetchScalarGridSpec(
                num_scalar_prefetch=1,
                grid=(slots,),
                in_specs=[pl.BlockSpec(shape, there if back else here)],
                out_specs=pl.BlockSpec(shape, here if back else there),
            ),
        )(q_owner, array)

    ordered = reordered(to_slots, response, response.dtype, False)
    dma = pltpu.SemaphoreType.DMA
    received = pl.pallas_call(
        functools.partial(team_kernel, pb, rows, team, tile),
        out_shape=jax.ShapeDtypeStruct((slots, 2, out_rows, size), BF16),
        in_specs=[pl.BlockSpec(memory_space=pl.ANY)] * 3,
        out_specs=pl.BlockSpec(memory_space=pl.ANY),
        scratch_shapes=[
            pltpu.VMEM((2, size, own_cols), BF16),
            pltpu.VMEM((2, size, size), BF16),
            pltpu.VMEM((2, size, own_cols), BF16),
            pltpu.VMEM((1, size), jnp.int32),
            pltpu.VMEM((team, rows, 2 * w_part, own_cols), BF16),
            pltpu.VMEM((max(team - 1, 1), rows, 2 * w_part, own_cols), BF16),
            pltpu.VMEM((rows, dests, 2, out_rows, size), BF16),
            dma((slots,)),
            dma((pb * spread,)),
            dma((per_pb * team,)),
            dma((rows,)),
            dma((rows * team,)),
            dma((rows * team,)),
            dma((team,)),
            dma(()),
            dma((rows * team,)),
            dma((rows * team,)),
            dma((rows * dests,)),
            dma((slots,)),
        ],
        compiler_params=pltpu.CompilerParams(
            collective_id=0, has_side_effects=True, vmem_limit_bytes=40 * 1024 * 1024
        ),
    )(ordered, screened, g_index.reshape(per_pb, 1, size))
    return reordered(from_slots, received, F32, True)


def solution(mesh):
    return jax.shard_map(
        functools.partial(body, mesh.shape["pb"], mesh.shape["row"]),
        mesh=mesh,
        in_specs=(P("pb", None, "row", None), P(None, None, "pb", "row"), P(), P("pb", None)),
        out_specs=P(None, None, ("row", "pb"), None),
        check_vma=False,
    )
```

time: 328 us -> 175 us (0.53)
  Pallas kernels: 0 us -> 169 us
  waiting for transfers between devices: 153 us -> 0 us
  local copies, waits for them, and re-layouts: 65.4 us -> 3.63 us
  blocking collectives: 52.8 us -> 0 us
  matrix products: 17.6 us -> 0 us
  between operations: 13.6 us -> 0.02 us
  starting transfers between devices: 11.5 us -> 0 us
  other arithmetic: 9.02 us -> 0 us
    pallas_call x0 -> x3, Pallas kernels: none -> 169 us  [the longest x1 148 us: body(): pl.pallas_call(functools.partial(team_kernel, pb, rows, team, tile), out_...]
    all_gather x1 -> x0, waiting for transfers between devices: 80.6 us -> none  [body(): whole = lax.all_gather(screened, 'row', axis=2, tiled=True)]
    all_to_all x2 -> x0, waiting for transfers between devices: 72.8 us -> none  [the longest x1 47.6 us: body(): lax.all_to_all(result, 'pb', split_axis=2, concat_axis=0, tiled=True)]
    all_to_all x1 -> x0, blocking collectives: 52.8 us -> none  [body(): lax.all_to_all(column_half, 'row', split_axis=2, concat_axis=3, tiled=True)]
    gather x4 -> x0, local copies, waits for them, and re-layouts: 32.1 us -> none  [the longest x2 25.2 us: body(): block[:, table, :]]
    all_to_all x6 -> x0, local copies, waits for them, and re-layouts: 18.4 us -> none  [the longest x2 6.94 us: body(): lax.all_to_all(result, 'pb', split_axis=2, concat_axis=0, tiled=True)]
    dot_general x8 -> x0, matrix products: 17.6 us -> none  [product(): jnp.einsum('qik,qkj->qij', first, second, preferred_element_type=jnp.floa...]
    all_to_all x2 -> x0, starting transfers between devices: 11.5 us -> none  [the longest x1 6.31 us: body(): lax.all_to_all(result, 'pb', split_axis=2, concat_axis=0, tiled=True)]
  transfers between devices with their start and end apart: 3 -> 0, of which waited for: 3 -> 0; matrix products, arithmetic and copies ran while one was open for 11% -> 0% of each run, Pallas kernels for 0% -> 0%
where the time goes in v1:
time: 175 us; the launch traced here: 172 us
  Pallas kernels  169 us (97%)
  local copies, waits for them, and re-layouts  3.63 us (2%)
    pallas_call x1, Pallas kernels, body(): pl.pallas_call(functools.partial(team_kernel, pb, rows, team, tile), out_...  148 us
    pallas_call x2, Pallas kernels, reordered(): pl.pallas_call(kernel, out_shape=jax.ShapeDtypeStruct(array.shape, dtype)...  20.8 us

profile of v1, /device:TPU:11, one launch (start us, length us, event | category | flops | bytes accessed | tf_op | source)
XLA Modules:
  0.0 172.2 jit_solution(6880331293953272355)
XLA Ops:
  0.0 0.7 reshape.3.table
  0.7 0.0 copy-start.2
  0.7 10.3 %shard_map.46.response = bf16[16,2,128,256]{3,2,1,0:T(8,128)(2,1)} custom-call(s32[16]{0:T(128)} %order.3, bf16[16,2,128,256]{3,2,1,0:T(8,128)(2,1)} %source.1), custom_call_target="tpu_custom_call" | custom-call | tf_op jit(solution)/shard_map/pallas_call | solution.py:292
  11.0 0.0 copy-done.2
  11.0 0.0 copy-start.1
  11.0 1.6 copy-done.1
  12.6 147.8 %shard_map.47.source = bf16[16,2,32,1024]{3,2,1,0:T(8,128)(2,1)S(1)} custom-call(bf16[16,2,128,256]{3,2,1,0:T(8,128)(2,1)S(1)} %copy-done.1, bf16[2,2,256,1024]{3,2,1,0:T(8,128)(2,1)S(1)} %copy-done.2, s32[2,1,1024]{2,1,0:T(1,128)S(1)} %reshape.3.table), custom_call_target="tpu_custom_call" | custom-call | tf_op jit(solution)/shard_map/pallas_call | solution.py:305
  160.4 0.0 copy-start
  160.4 1.3 copy-done
  161.7 10.5 %shard_map.48 = f32[16,2,32,1024]{3,2,1,0:T(8,128)} custom-call(s32[16]{0:T(128)} %order.3, bf16[16,2,32,1024]{3,2,1,0:T(8,128)(2,1)} %copy-done), custom_call_target="tpu_custom_call" | custom-call | tf_op jit(solution)/shard_map/pallas_call | solution.py:292
Async XLA Ops:
  0.7 10.3 %copy-start.2 = (bf16[2,2,256,1024]{3,2,1,0:T(8,128)(2,1)S(1)}, bf16[2,2,256,1024]{3,2,1,0:T(8,128)(2,1)}, u32[]{:S(2)}) copy-start(bf16[2,2,256,1024]{3,2,1,0:T(8,128)(2,1)} %screened.1) | copy-start | bytes 6291460
  11.0 1.6 copy-start.1
  160.4 1.3 copy-start

commit v2 on v1

--- a/solution.py
+++ b/solution.py
@@ -11,19 +11,16 @@
 BF16 = jnp.bfloat16
 
 
-def to_slots(order, source, target):
-    target[...] = source[...]
-
-
-def from_slots(order, source, target):
-    target[...] = source[...].astype(target.dtype)
+def from_slots(count, order, source, target):
+    for i in range(count):
+        target[i] = source[order[pl.program_id(0) * count + i]].astype(target.dtype)
 
 
 def team_kernel(
     pb, rows, team, tile,
-    response, screened, table, out,
-    raw, weight, chi, owner_table, half, half_out, stage,
-    chi_sent, chi_got, w_sent, w_got, f_sent, f_got, g_sent, g_got, h_sent, h_got, o_sent, o_got,
+    order, unordered, screened, table, out,
+    loaded, response, own_table, raw, weight, chi, owner_table, half, half_out, stage,
+    load_got, chi_sent, chi_got, w_sent, w_got, f_sent, f_got, g_sent, g_got, h_sent, h_got, o_sent, o_got,
 ):
     slots = response.shape[0]
     per_pb = screened.shape[0]
@@ -45,6 +42,8 @@
     def same(a, b):
         return jnp.logical_and(a == p, b == r)
 
+    load = pltpu.make_async_copy(unordered, loaded, load_got)
+    load.start()
     barrier = pltpu.get_barrier_semaphore()
 
     def greet(k, carry):
@@ -54,6 +53,22 @@
         return carry
 
     lax.fori_loop(0, pb * rows, greet, 0)
+
+    for i in range(per_pb):
+        @pl.when(r % per_pb == i)
+        def _():
+            own_table[...] = table[i : i + 1, :]
+
+    load.wait()
+
+    def arrange(number, carry):
+        q = 0
+        for i in range(1, slots):
+            q = jnp.where(order[i] == number, i, q)
+        response[number] = loaded[q]
+        return carry
+
+    lax.fori_loop(0, slots, arrange, 0)
     pl.semaphore_wait(barrier, pb * rows - 1)
 
     def send(src, dst, sent, got, at_p, at_r):
@@ -86,13 +101,11 @@
         return jnp.where(k < near, across, beside)
 
     holder = r // per_pb
-    mine = table.at[r % per_pb]
-
     @pl.when(t == holder)
     def _():
-        pltpu.make_async_copy(mine, owner_table, g_got).start()
-        for step in range(1, team):
-            remote(mine, owner_table, g_sent.at[step - 1], g_got, group * team + (t + step) % team, r).start()
+        pltpu.make_async_copy(own_table, owner_table, g_got).start()
+        for step in range(1, team):
+            remote(own_table, owner_table, g_sent.at[step - 1], g_got, group * team + (t + step) % team, r).start()
 
     member = r // spread
 
@@ -156,12 +169,12 @@
         ref = w_target(block, t)
         return remote(ref, ref, f_sent.at[block * team + step], f_got.at[block * team + step], at_p, r)
 
-    def pass_on(k, carry):
-        block = (r + k) % rows
+    def take(block):
         arrived(w_target(block, t), w_got.at[block])
         for step in range(1, team):
             forward(block, step).start()
-        return carry
+        for step in range(1, team):
+            arrived(w_target(block, (t + team - step) % team), f_got.at[block * team + step])
 
     def hand(block, step):
         at_p = group * team + (t + step) % team
@@ -172,12 +185,8 @@
 
     width = min(tile, own_cols)
 
-    def first(k, carry):
-        block = (r + k) % rows
-        pass_on(k, carry)
-        for step in range(1, team):
-            arrived(w_target(block, (t + team - step) % team), f_got.at[block * team + step])
-        for step in range(team):
+    def first(block):
+        for step in range(1, team + 1):
             part = (t + step) % team
             start = pl.multiple_of(block * w_rows + part * w_part, w_part)
             both = jnp.concatenate(
@@ -190,21 +199,18 @@
                 real = (by_real[:w_part] - by_imag[w_part:]).astype(BF16)
                 imag = (by_imag[:w_part] + by_real[w_part:]).astype(BF16)
                 value = jnp.concatenate((real, imag), axis=0)
-                if step == 0:
+                if step == team:
                     half[t, block, :, cols] = value
                 else:
                     half_out[step - 1, block, :, cols] = value
-        for step in range(1, team):
-            hand(block, step).start()
-        return carry
-
-    lax.fori_loop(0, rows, first, 0)
+            if step < team:
+                hand(block, step).start()
 
     def out_send(k, m):
         at_r = far_first(k)
         send(stage.at[at_r, m], out.at[slot], o_sent.at[at_r * dests + m], o_got.at[slot], t * dests + m, at_r)
 
-    def second(k, carry):
+    def second(k):
         block = far_first(k)
         for step in range(1, team):
             arrived(half.at[(t + team - step) % team, block], h_got.at[block * team + step])
@@ -228,15 +234,27 @@
 
         lax.fori_loop(0, size // tile, columns, 0)
 
-        @pl.when(k > 0)
-        def _():
-            for m in range(dests):
-                out_send(k - 1, m)
-        return carry
-
-    lax.fori_loop(0, rows, second, 0)
-    for m in range(dests):
-        out_send(rows - 1, m)
+        for m in range(dests):
+            out_send(k, m)
+
+    def near_first(k, carry):
+        block = far_first(rows - 1 - k)
+        take(block)
+        first(block)
+        return carry
+
+    lax.fori_loop(0, rows - 1, near_first, 0)
+    take(far_first(0))
+
+    def finish(k, carry):
+        @pl.when(k == 1)
+        def _():
+            first(far_first(0))
+
+        second(jnp.where(k < 2, 1 - k, k))
+        return carry
+
+    lax.fori_loop(0, rows, finish, 0)
 
     def out_wait(k, carry):
         arrived(out.at[k], o_got.at[k])
@@ -247,7 +265,7 @@
     @pl.when(t == holder)
     def _():
         for step in range(1, team):
-            pltpu.make_async_copy(mine, mine, g_sent.at[step - 1]).wait()
+            pltpu.make_async_copy(own_table, own_table, g_sent.at[step - 1]).wait()
 
     def chi_left(k, carry):
         number, at_p, at_r = chi_place(k)
@@ -285,29 +303,21 @@
     spread = rows // team
     tile = min(256, size)
 
-    def reordered(kernel, array, dtype, back):
-        shape = (1,) + array.shape[1:]
-        here = lambda q, order: (q, 0, 0, 0)
-        there = lambda q, order: (order[q], 0, 0, 0)
-        return pl.pallas_call(
-            kernel,
-            out_shape=jax.ShapeDtypeStruct(array.shape, dtype),
-            grid_spec=pltpu.PrefetchScalarGridSpec(
-                num_scalar_prefetch=1,
-                grid=(slots,),
-                in_specs=[pl.BlockSpec(shape, there if back else here)],
-                out_specs=pl.BlockSpec(shape, here if back else there),
-            ),
-        )(q_owner, array)
-
-    ordered = reordered(to_slots, response, response.dtype, False)
     dma = pltpu.SemaphoreType.DMA
     received = pl.pallas_call(
         functools.partial(team_kernel, pb, rows, team, tile),
         out_shape=jax.ShapeDtypeStruct((slots, 2, out_rows, size), BF16),
-        in_specs=[pl.BlockSpec(memory_space=pl.ANY)] * 3,
+        in_specs=[
+            pl.BlockSpec(memory_space=pltpu.SMEM),
+            pl.BlockSpec(memory_space=pl.ANY),
+            pl.BlockSpec(memory_space=pl.ANY),
+            pl.BlockSpec(memory_space=pltpu.VMEM),
+        ],
         out_specs=pl.BlockSpec(memory_space=pl.ANY),
         scratch_shapes=[
+            pltpu.VMEM(response.shape, BF16),
+            pltpu.VMEM(response.shape, BF16),
+            pltpu.VMEM((1, size), jnp.int32),
             pltpu.VMEM((2, size, own_cols), BF16),
             pltpu.VMEM((2, size, size), BF16),
             pltpu.VMEM((2, size, own_cols), BF16),
@@ -315,6 +325,7 @@
             pltpu.VMEM((team, rows, 2 * w_part, own_cols), BF16),
             pltpu.VMEM((max(team - 1, 1), rows, 2 * w_part, own_cols), BF16),
             pltpu.VMEM((rows, dests, 2, out_rows, size), BF16),
+            dma(()),
             dma((slots,)),
             dma((pb * spread,)),
             dma((per_pb * team,)),
@@ -329,10 +340,20 @@
             dma((slots,)),
         ],
         compiler_params=pltpu.CompilerParams(
-            collective_id=0, has_side_effects=True, vmem_limit_bytes=40 * 1024 * 1024
+            collective_id=0, has_side_effects=True, vmem_limit_bytes=60 * 1024 * 1024
         ),
-    )(ordered, screened, g_index.reshape(per_pb, 1, size))
-    return reordered(from_slots, received, F32, True)
+    )(q_owner, response, screened, g_index)
+    count = slots // 4
+    return pl.pallas_call(
+        functools.partial(from_slots, count),
+        out_shape=jax.ShapeDtypeStruct(received.shape, F32),
+        grid_spec=pltpu.PrefetchScalarGridSpec(
+            num_scalar_prefetch=1,
+            grid=(slots // count,),
+            in_specs=[pl.BlockSpec(received.shape, lambda q, order: (0, 0, 0, 0), pipeline_mode=pl.Buffered(1))],
+            out_specs=pl.BlockSpec((count,) + received.shape[1:], lambda q, order: (q, 0, 0, 0)),
+        ),
+    )(q_owner, received)
 
 
 def solution(mesh):

time: 175 us -> 173 us (0.989)
  the two profiles are of different devices: /device:TPU:11 before, /device:TPU:19 now
where the time goes in v2:
time: 173 us
  Pallas kernels  173 us (100%)
    pallas_call x1, Pallas kernels, body(): pl.pallas_call(functools.partial(team_kernel, pb, rows, team, tile), out_...  168 us
    pallas_call x1, Pallas kernels, body(): pl.pallas_call(functools.partial(from_slots, count), out_shape=jax.ShapeD...  4.7 us

profile of v2, /device:TPU:19, one launch (start us, length us, event | category | flops | bytes accessed | tf_op | source)
XLA Modules:
  0.0 172.7 jit_solution(7058380094122324780)
XLA Ops:
  0.0 168.0 %shard_map.46.source = bf16[16,2,32,1024]{3,2,1,0:T(8,128)(2,1)} custom-call(s32[16]{0:T(128)} %order.3, bf16[16,2,128,256]{3,2,1,0:T(8,128)(2,1)} %unordered.1, bf16[2,2,256,1024]{3,2,1,0:T(8,128)(2,1)} %screened.1, s32[2,1024]{1,0:T(2,128)} %table.1), custom_call_target="tpu_custom_call" | custom-call | tf_op jit(solution)/shard_map/pallas_call | solution.py:307
  168.0 4.7 %shard_map.47 = f32[16,2,32,1024]{3,2,1,0:T(8,128)} custom-call(s32[16]{0:T(128)} %order.3, bf16[16,2,32,1024]{3,2,1,0:T(8,128)(2,1)} %shard_map.46.source), custom_call_target="tpu_custom_call" | custom-call | tf_op jit(solution)/shard_map/pallas_call | solution.py:347

commit v3 on v2

--- a/solution.py
+++ b/solution.py
@@ -107,6 +107,23 @@
         for step in range(1, team):
             remote(own_table, owner_table, g_sent.at[step - 1], g_got, group * team + (t + step) % team, r).start()
 
+    def w_target(block, part):
+        start = pl.multiple_of(block * w_rows + part * w_part, w_part)
+        return weight.at[:, pl.ds(start, w_part), :]
+
+    def w_place(k):
+        i, part = k // team, k % team
+        return i, part, group * team + part, t * per_pb + i
+
+    def w_send(k, carry):
+        i, part, at_p, at_r = w_place(k)
+        src = screened.at[i, :, pl.ds(pl.multiple_of(part * w_part, w_part), w_part), :]
+        send(src, w_target(r, part), w_sent.at[k], w_got.at[r], at_p, at_r)
+        return carry
+
+
+    lax.fori_loop(0, per_pb * team, w_send, 0)
+
     member = r // spread
 
     def chi_place(k):
@@ -127,22 +144,6 @@
         return carry
 
     lax.fori_loop(0, slots, chi_send, 0)
-
-    def w_target(block, part):
-        start = pl.multiple_of(block * w_rows + part * w_part, w_part)
-        return weight.at[:, pl.ds(start, w_part), :]
-
-    def w_place(k):
-        i, part = k // team, k % team
-        return i, part, group * team + part, t * per_pb + i
-
-    def w_send(k, carry):
-        i, part, at_p, at_r = w_place(k)
-        src = screened.at[i, :, pl.ds(pl.multiple_of(part * w_part, w_part), w_part), :]
-        send(src, w_target(r, part), w_sent.at[k], w_got.at[r], at_p, at_r)
-        return carry
-
-    lax.fori_loop(0, per_pb * team, w_send, 0)
 
     arrived(owner_table, g_got)
 
@@ -206,11 +207,19 @@
             if step < team:
                 hand(block, step).start()
 
+    def in_turn(k, carry):
+        block = (r + k) % rows
+        take(block)
+        first(block)
+        return carry
+
+    lax.fori_loop(0, rows, in_turn, 0)
+
     def out_send(k, m):
         at_r = far_first(k)
         send(stage.at[at_r, m], out.at[slot], o_sent.at[at_r * dests + m], o_got.at[slot], t * dests + m, at_r)
 
-    def second(k):
+    def second(k, carry):
         block = far_first(k)
         for step in range(1, team):
             arrived(half.at[(t + team - step) % team, block], h_got.at[block * team + step])
@@ -234,27 +243,15 @@
 
         lax.fori_loop(0, size // tile, columns, 0)
 
-        for m in range(dests):
-            out_send(k, m)
-
-    def near_first(k, carry):
-        block = far_first(rows - 1 - k)
-        take(block)
-        first(block)
-        return carry
-
-    lax.fori_loop(0, rows - 1, near_first, 0)
-    take(far_first(0))
-
-    def finish(k, carry):
-        @pl.when(k == 1)
-        def _():
-            first(far_first(0))
-
-        second(jnp.where(k < 2, 1 - k, k))
-        return carry
-
-    lax.fori_loop(0, rows, finish, 0)
+        @pl.when(k > 0)
+        def _():
+            for m in range(dests):
+                out_send(k - 1, m)
+        return carry
+
+    lax.fori_loop(0, rows, second, 0)
+    for m in range(dests):
+        out_send(rows - 1, m)
 
     def out_wait(k, carry):
         arrived(out.at[k], o_got.at[k])

time: 173 us -> 166 us (0.960)
  the two profiles are of different devices: /device:TPU:19 before, /device:TPU:11 now
where the time goes in v3:
time: 166 us; the launch traced here: 165 us
  Pallas kernels  165 us (99%)
    pallas_call x1, Pallas kernels, body(): pl.pallas_call(functools.partial(team_kernel, pb, rows, team, tile), out_...  161 us
    pallas_call x1, Pallas kernels, body(): pl.pallas_call(functools.partial(from_slots, count), out_shape=jax.ShapeD...  4.7 us

profile of v3, /device:TPU:11, one launch (start us, length us, event | category | flops | bytes accessed | tf_op | source)
XLA Modules:
  0.0 165.4 jit_solution(5739919979846834877)
XLA Ops:
  0.0 160.6 %shard_map.46.source = bf16[16,2,32,1024]{3,2,1,0:T(8,128)(2,1)} custom-call(s32[16]{0:T(128)} %order.3, bf16[16,2,128,256]{3,2,1,0:T(8,128)(2,1)} %unordered.1, bf16[2,2,256,1024]{3,2,1,0:T(8,128)(2,1)} %screened.1, s32[2,1024]{1,0:T(2,128)} %table.1), custom_call_target="tpu_custom_call" | custom-call | tf_op jit(solution)/shard_map/pallas_call | solution.py:304
  160.7 4.7 %shard_map.47 = f32[16,2,32,1024]{3,2,1,0:T(8,128)} custom-call(s32[16]{0:T(128)} %order.3, bf16[16,2,32,1024]{3,2,1,0:T(8,128)(2,1)} %shard_map.46.source), custom_call_target="tpu_custom_call" | custom-call | tf_op jit(solution)/shard_map/pallas_call | solution.py:344

commit v4 on v3

--- a/solution.py
+++ b/solution.py
@@ -19,7 +19,7 @@
 def team_kernel(
     pb, rows, team, tile,
     order, unordered, screened, table, out,
-    loaded, response, own_table, raw, weight, chi, owner_table, half, half_out, stage,
+    loaded, response, own_table, raw, weight, turned, owner_table, half, half_out, stage,
     load_got, chi_sent, chi_got, w_sent, w_got, f_sent, f_got, g_sent, g_got, h_sent, h_got, o_sent, o_got,
 ):
     slots = response.shape[0]
@@ -145,26 +145,6 @@
 
     lax.fori_loop(0, slots, chi_send, 0)
 
-    arrived(owner_table, g_got)
-
-    def chi_wait(k, carry):
-        arrived(chi_target(k // spread, k % spread), chi_got.at[k])
-        return carry
-
-    lax.fori_loop(0, pb * spread, chi_wait, 0)
-
-    def reorder(k, carry):
-        start = pl.multiple_of(k * tile, tile)
-        wanted = owner_table[:, pl.ds(start, tile)]
-        chosen = (lax.broadcasted_iota(jnp.int32, (size, tile), 0) == wanted).astype(F32).astype(BF16)
-        for part in range(2):
-            chi[part, pl.ds(start, tile), :] = lax.dot_general(
-                chosen, raw[part], (((0,), (0,)), ((), ())), preferred_element_type=F32
-            ).astype(BF16)
-        return carry
-
-    lax.fori_loop(0, size // tile, reorder, 0)
-
     def forward(block, step):
         at_p = group * team + (t + step) % team
         ref = w_target(block, t)
@@ -186,17 +166,41 @@
 
     width = min(tile, own_cols)
 
+    def take_turn(k, carry):
+        take((r + k) % rows)
+        return carry
+
+    lax.fori_loop(0, rows, take_turn, 0)
+    arrived(owner_table, g_got)
+
+    def reorder(k, carry):
+        start = pl.multiple_of((k // 2) * tile, tile)
+        wanted = lax.broadcasted_iota(jnp.int32, (tile, size), 0) + start
+        chosen = (wanted == owner_table[...]).astype(F32).astype(BF16)
+        turned[k % 2, :, pl.ds(start, tile)] = lax.dot_general(
+            weight[k % 2], chosen, (((1,), (1,)), ((), ())), preferred_element_type=F32
+        ).astype(BF16)
+        return carry
+
+    lax.fori_loop(0, 2 * (size // tile), reorder, 0)
+
+    def chi_wait(k, carry):
+        arrived(chi_target(k // spread, k % spread), chi_got.at[k])
+        return carry
+
+    lax.fori_loop(0, pb * spread, chi_wait, 0)
+
     def first(block):
         for step in range(1, team + 1):
             part = (t + step) % team
             start = pl.multiple_of(block * w_rows + part * w_part, w_part)
             both = jnp.concatenate(
-                (weight[0, pl.ds(start, w_part), :], weight[1, pl.ds(start, w_part), :]), axis=0
+                (turned[0, pl.ds(start, w_part), :], turned[1, pl.ds(start, w_part), :]), axis=0
             )
             for c in range(own_cols // width):
                 cols = slice(c * width, (c + 1) * width)
-                by_real = jnp.dot(both, chi[0, :, cols], preferred_element_type=F32)
-                by_imag = jnp.dot(both, chi[1, :, cols], preferred_element_type=F32)
+                by_real = jnp.dot(both, raw[0, :, cols], preferred_element_type=F32)
+                by_imag = jnp.dot(both, raw[1, :, cols], preferred_element_type=F32)
                 real = (by_real[:w_part] - by_imag[w_part:]).astype(BF16)
                 imag = (by_imag[:w_part] + by_real[w_part:]).astype(BF16)
                 value = jnp.concatenate((real, imag), axis=0)
@@ -209,7 +213,6 @@
 
     def in_turn(k, carry):
         block = (r + k) % rows
-        take(block)
         first(block)
         return carry
 
@@ -317,7 +320,7 @@
             pltpu.VMEM((1, size), jnp.int32),
             pltpu.VMEM((2, size, own_cols), BF16),
             pltpu.VMEM((2, size, size), BF16),
-            pltpu.VMEM((2, size, own_cols), BF16),
+            pltpu.VMEM((2, size, size), BF16),
             pltpu.VMEM((1, size), jnp.int32),
             pltpu.VMEM((team, rows, 2 * w_part, own_cols), BF16),
             pltpu.VMEM((max(team - 1, 1), rows, 2 * w_part, own_cols), BF16),

time: 166 us -> 159 us (0.958)
  Pallas kernels: 165 us -> 159 us
    pallas_call x1, Pallas kernels: 161 us -> 154 us  [body(): pl.pallas_call(functools.partial(team_kernel, pb, rows, team, tile), out_...]
where the time goes in v4:
time: 159 us
  Pallas kernels  159 us (100%)
    pallas_call x1, Pallas kernels, body(): pl.pallas_call(functools.partial(team_kernel, pb, rows, team, tile), out_...  154 us
    pallas_call x1, Pallas kernels, body(): pl.pallas_call(functools.partial(from_slots, count), out_shape=jax.ShapeD...  4.7 us

profile of v4, /device:TPU:11, one launch (start us, length us, event | category | flops | bytes accessed | tf_op | source)
XLA Modules:
  0.0 158.6 jit_solution(13093300379831083631)
XLA Ops:
  0.0 153.9 %shard_map.46.source = bf16[16,2,32,1024]{3,2,1,0:T(8,128)(2,1)} custom-call(s32[16]{0:T(128)} %order.3, bf16[16,2,128,256]{3,2,1,0:T(8,128)(2,1)} %unordered.1, bf16[2,2,256,1024]{3,2,1,0:T(8,128)(2,1)} %screened.1, s32[2,1024]{1,0:T(2,128)} %table.1), custom_call_target="tpu_custom_call" | custom-call | tf_op jit(solution)/shard_map/pallas_call | solution.py:307
  153.9 4.7 %shard_map.47 = f32[16,2,32,1024]{3,2,1,0:T(8,128)} custom-call(s32[16]{0:T(128)} %order.3, bf16[16,2,32,1024]{3,2,1,0:T(8,128)(2,1)} %shard_map.46.source), custom_call_target="tpu_custom_call" | custom-call | tf_op jit(solution)/shard_map/pallas_call | solution.py:347

commit v5 on v4

--- a/solution.py
+++ b/solution.py
@@ -164,8 +164,6 @@
             h_sent.at[block * team + step], h_got.at[block * team + step], at_p, r,
         )
 
-    width = min(tile, own_cols)
-
     def take_turn(k, carry):
         take((r + k) % rows)
         return carry
@@ -184,21 +182,14 @@
 
     lax.fori_loop(0, 2 * (size // tile), reorder, 0)
 
-    def chi_wait(k, carry):
-        arrived(chi_target(k // spread, k % spread), chi_got.at[k])
-        return carry
-
-    lax.fori_loop(0, pb * spread, chi_wait, 0)
-
-    def first(block):
+    def first(block, c):
         for step in range(1, team + 1):
             part = (t + step) % team
             start = pl.multiple_of(block * w_rows + part * w_part, w_part)
             both = jnp.concatenate(
                 (turned[0, pl.ds(start, w_part), :], turned[1, pl.ds(start, w_part), :]), axis=0
             )
-            for c in range(own_cols // width):
-                cols = slice(c * width, (c + 1) * width)
+            for cols in (slice(c * block_cols, (c + 1) * block_cols),):
                 by_real = jnp.dot(both, raw[0, :, cols], preferred_element_type=F32)
                 by_imag = jnp.dot(both, raw[1, :, cols], preferred_element_type=F32)
                 real = (by_real[:w_part] - by_imag[w_part:]).astype(BF16)
@@ -208,15 +199,20 @@
                     half[t, block, :, cols] = value
                 else:
                     half_out[step - 1, block, :, cols] = value
-            if step < team:
+            if step < team and c == spread - 1:
                 hand(block, step).start()
 
-    def in_turn(k, carry):
-        block = (r + k) % rows
-        first(block)
-        return carry
-
-    lax.fori_loop(0, rows, in_turn, 0)
+    for c in range(spread):
+        def chi_wait(k, carry):
+            arrived(chi_target(k, c), chi_got.at[k * spread + c])
+            return carry
+
+        def in_turn(k, carry):
+            first((r + k) % rows, c)
+            return carry
+
+        lax.fori_loop(0, pb, chi_wait, 0)
+        lax.fori_loop(0, rows, in_turn, 0)
 
     def out_send(k, m):
         at_r = far_first(k)

time: 159 us -> 161 us (1.013)
  Pallas kernels: 159 us -> 161 us
    pallas_call x1, Pallas kernels: 154 us -> 156 us  [body(): pl.pallas_call(functools.partial(team_kernel, pb, rows, team, tile), out_...]
where the time goes in v5:
time: 161 us
  Pallas kernels  161 us (100%)
    pallas_call x1, Pallas kernels, body(): pl.pallas_call(functools.partial(team_kernel, pb, rows, team, tile), out_...  156 us
    pallas_call x1, Pallas kernels, body(): pl.pallas_call(functools.partial(from_slots, count), out_shape=jax.ShapeD...  4.7 us

profile of v5, /device:TPU:11, one launch (start us, length us, event | category | flops | bytes accessed | tf_op | source)
XLA Modules:
  0.0 160.6 jit_solution(17634021747273636626)
XLA Ops:
  0.0 155.9 %shard_map.46.source = bf16[16,2,32,1024]{3,2,1,0:T(8,128)(2,1)} custom-call(s32[16]{0:T(128)} %order.3, bf16[16,2,128,256]{3,2,1,0:T(8,128)(2,1)} %unordered.1, bf16[2,2,256,1024]{3,2,1,0:T(8,128)(2,1)} %screened.1, s32[2,1024]{1,0:T(2,128)} %table.1), custom_call_target="tpu_custom_call" | custom-call | tf_op jit(solution)/shard_map/pallas_call | solution.py:303
  155.9 4.7 %shard_map.47 = f32[16,2,32,1024]{3,2,1,0:T(8,128)} custom-call(s32[16]{0:T(128)} %order.3, bf16[16,2,32,1024]{3,2,1,0:T(8,128)(2,1)} %shard_map.46.source), custom_call_target="tpu_custom_call" | custom-call | tf_op jit(solution)/shard_map/pallas_call | solution.py:343
